TPU v7x, 128 devices: a whole 4x4x4 slice. The times are simulated.
128 devices in a mesh: cand: 16 (over z_lo, y, core), rel: 8 (over z_hi, x).
Axes of the slice: x: 4, y: 4, z: 4 (z_hi: 2, z_lo: 2; z = z_hi * 2 + z_lo), core: 2. Of those that a mesh axis runs over, the one named last changes fastest.
Arguments:
- source_rows: bfloat16 [262144, 512], P(('cand', 'rel')), may hold values from -24 to 24
- rel_ids: int32 [262144, 1], P(('cand', 'rel')), may hold values from 0 to 15; in each aligned block of 2048 rows (0 to 2047, 2048 to 4095, ...) at most 256 rows name the same one
- relations: bfloat16 [16, 512, 512], P('rel'), may hold values from -0.25 to 0.25
- entities: float32 [32768, 512], P(('cand', 'rel')), may hold values from -0.3 to 0.3
- pos_slot: int32 [262144], P(('cand', 'rel')), may hold values from 0 to 2047
- negatives: int32 [8, 262144, 16], P(None, ('cand', 'rel')), may hold values from 0 to 255
Outputs:
- updated_entities: float32 [32768, 512], P(('cand', 'rel'))
- source_grad: bfloat16 [262144, 512], P(('cand', 'rel'))
- relation_grad: float32 [512, 16, 512], P('cand', 'rel')
Inputs may be any that keep to these rules, and one draw needn't show every extreme that they name: `rel_ids`: in each aligned block of 2048 rows (the rows of one device) no relation is named by more than 256 rows, a bound that some block reaches.
All inputs are finite; a program needn't handle non-finite values.
Results may differ from a plain program's by a relative error of at most 0.019.
Values may be sent and summed in bfloat16 or wider, within the bound.
A program may use at most 128 MiB of HBM per device.

v0:
```python
import jax
import jax.numpy as jnp
from jax import lax
from jax.sharding import PartitionSpec as P

STOPS = 8
learn_rate = 0.005


def from_behind(block, axis, distance):
    devices = range(lax.axis_size(axis))
    route = [((i - distance) % len(devices), i) for i in devices]
    return lax.ppermute(block, axis, route)


def slot_index(rel_ids, nrel, most):
    ids = rel_ids[:, 0]
    onehot = (ids[:, None] == jnp.arange(nrel, dtype=jnp.int32)[None, :]).astype(jnp.int32)
    rank = jnp.cumsum(onehot, axis=0) - onehot
    return ids * most + jnp.sum(rank * onehot, axis=1)


def place_rows(rows, slot, total):
    return jnp.zeros((total, rows.shape[1]), rows.dtype).at[slot].set(rows)


def shards(source_rows, rel_ids, relations, entities, pos_slot, negatives):
    src_rows, width = source_rows.shape
    rel_dev = relations.shape[0]
    owners = lax.axis_size("rel")
    nrel = rel_dev * owners
    most = 2 * src_rows // nrel
    slot = slot_index(rel_ids, nrel, most)
    sent = place_rows(source_rows, slot, nrel * most).reshape(nrel, most, width)
    every_matrix = lax.all_gather(relations, "rel", axis=0, tiled=True)
    q_slots = jnp.einsum(
        "kmd,kde->kme", sent, every_matrix, preferred_element_type=jnp.float32
    ).astype(jnp.bfloat16)
    queries = q_slots.reshape(nrel * most, width)[slot]
    part_rows = entities.shape[0]
    columns = jnp.arange(part_rows, dtype=jnp.int32)
    state = entities
    query_acc = jnp.zeros((src_rows, width), jnp.float32)
    for stop in range(STOPS):
        if stop > 0:
            state = from_behind(state, "cand", 1)
        wide = state.astype(jnp.bfloat16)
        logits = lax.dot_general(
            queries, wide, (((1,), (1,)), ((), ())), preferred_element_type=jnp.float32
        )
        picks = negatives[stop]
        counts = jnp.zeros(logits.shape, jnp.float32)
        for sample in range(picks.shape[1]):
            counts = counts + (picks[:, sample][:, None] == columns[None, :]).astype(jnp.float32)
        hits = (pos_slot[:, None] == stop * part_rows + columns[None, :]).astype(jnp.float32)
        weight = (counts * jax.nn.sigmoid(logits) - hits * jax.nn.sigmoid(-logits)).astype(
            jnp.bfloat16
        )
        query_acc = query_acc + jnp.dot(weight, wide, preferred_element_type=jnp.float32)
        change = lax.dot_general(
            weight, queries, (((0,), (0,)), ((), ())), preferred_element_type=jnp.float32
        )
        state = state - learn_rate * change
    query_grad = query_acc.astype(jnp.bfloat16)
    gq_slots = place_rows(query_grad, slot, nrel * most).reshape(nrel, most, width)
    back_slots = jnp.einsum(
        "kme,kde->kmd", gq_slots, every_matrix, preferred_element_type=jnp.float32
    ).astype(jnp.bfloat16)
    terms = jnp.einsum("kmd,kme->dke", sent, gq_slots, preferred_element_type=jnp.float32)
    partial_value = lax.psum_scatter(
        terms.astype(jnp.bfloat16), "rel", scatter_dimension=1, tiled=True
    )
    source_grad = back_slots.reshape(nrel * most, width)[slot]
    relation_grad = lax.psum_scatter(partial_value, "cand", scatter_dimension=0, tiled=True).astype(
        jnp.float32
    )
    return (state, source_grad, relation_grad)


def solution(mesh):
    placed = (
        P(("cand", "rel"), None),
        P(("cand", "rel"), None),
        P("rel", None, None),
        P(("cand", "rel"), None),
        P(("cand", "rel")),
        P(None, ("cand", "rel"), None),
    )
    return jax.shard_map(
        shards,
        mesh=mesh,
        in_specs=placed,
        out_specs=(P(("cand", "rel"), None), P(("cand", "rel"), None), P("cand", "rel", None)),
        check_vma=False,
    )
```

profile of v0, /device:TPU:1, one launch (start us, length us, event | category | flops | bytes accessed | tf_op | source)
XLA Modules:
  0.0 535.6 jit_solution(7300290726071133954)
XLA Ops:
  7.2 0.7 all-gather.2.cloned.1.call-update
  7.9 0.7 fusion.63
  8.7 4.5 reduce-window.6
  13.2 0.4 slice_reduce_fusion
  13.9 0.8 fusion.14
  14.7 0.7 compare_select_fusion
  15.4 12.6 %scatter_custom_fusion = bf16[4096,512]{1,0:T(8,128)(2,1)} fusion(s32[2048]{0:T(1024)S(1)} %bitcast.221, bf16[2048,512]{1,0:T(8,128)(2,1)} %param.6, bf16[]{:T(256)} %constant.14.clone.1), kind=kCustom, calls=%fused_computation.131 | custom fusion | bytes 4194816 | tf_op jit(solution)/shard_map/scatter | solution.py:24
  28.1 0.6 iota_add_fusion.6
  28.6 0.6 iota_add_fusion.5
  29.4 0.7 fusion.70
  30.2 0.7 fusion.69
  30.9 0.7 fusion.68
  31.6 0.7 fusion.67
  32.4 88.9 %all-gather.2.cloned.1.call-done = bf16[16,512,512]{2,1,0:T(8,128)(2,1)} async-done(((bf16[2,512,512]{2,1,0:T(8,128)(2,1)}), bf16[16,512,512]{2,1,0:T(8,128)(2,1)}) %all-gather.2.cloned.1.call-update) | async-done | bytes 8388624 | tf_op jit(solution)/shard_map/all_gather | solution.py:35
  121.2 9.2 %convolution_convert_fusion.1 = bf16[16,256,512]{2,1,0:T(8,128)(2,1)} fusion(bf16[16,256,512]{2,1,0:T(8,128)(2,1)} %bitcast.213, bf16[16,512,512]{2,1,0:T(8,128)(2,1)} %all-gather.2.cloned.1.call-done), kind=kOutput, calls=%fused_computation.7 | convolution fusion | flops 2149580800 | bytes 16777216 | tf_op jit(solution)/shard_map/kmd,kde->kme/dot_general | solution.py:36
  130.4 10.4 %gather_fusion = bf16[2048,512]{1,0:T(8,128)(2,1)S(1)} fusion(bf16[4096,512]{1,0:T(8,128)(2,1)} %bitcast.211, s32[2048]{0:T(1024)S(1)} %broadcast_clamp_fusion), kind=kCustom, calls=%fused_computation | custom fusion | bytes 4202496 | tf_op jit(solution)/shard_map/gather | solution.py:39
  140.8 5.2 subtract_convert_fusion.7
  146.2 0.7 fusion.11
  147.0 3.1 collective-permute-start
  150.1 6.0 %collective-permute-done = f32[256,512]{1,0:T(8,128)S(1)} collective-permute-done((f32[256,512]{1,0:T(8,128)S(1)}, f32[256,512]{1,0:T(8,128)S(1)}, u32[]{:S(2)}, u32[]{:S(2)}) %collective-permute-start) | collective-permute-done | bytes 524320 | tf_op jit(solution)/shard_map/ppermute | solution.py:13
  156.3 5.2 subtract_convert_fusion.6
  161.7 0.7 fusion.10
  162.4 2.6 collective-permute-start.1
  165.1 6.0 %collective-permute-done.1 = f32[256,512]{1,0:T(8,128)S(1)} collective-permute-done((f32[256,512]{1,0:T(8,128)S(1)}, f32[256,512]{1,0:T(8,128)S(1)}, u32[]{:S(2)}, u32[]{:S(2)}) %collective-permute-start.1) | collective-permute-done | bytes 524320 | tf_op jit(solution)/shard_map/ppermute | solution.py:13
  171.2 5.2 subtract_convert_fusion.5
  176.6 0.7 fusion.9
  177.3 2.6 collective-permute-start.2
  180.0 6.0 %collective-permute-done.2 = f32[256,512]{1,0:T(8,128)S(1)} collective-permute-done((f32[256,512]{1,0:T(8,128)S(1)}, f32[256,512]{1,0:T(8,128)S(1)}, u32[]{:S(2)}, u32[]{:S(2)}) %collective-permute-start.2) | collective-permute-done | bytes 524320 | tf_op jit(solution)/shard_map/ppermute | solution.py:13
  186.2 5.2 subtract_convert_fusion.4
  191.3 0.7 fusion.8
  192.1 2.6 collective-permute-start.3
  194.8 2.8 fusion.57
  197.6 3.7 collective-permute-done.3
  201.4 5.2 subtract_convert_fusion.3
  206.6 0.7 fusion.7
  207.3 2.2 collective-permute-start.4
  209.6 2.7 fusion.51
  212.2 2.8 fusion.45
  215.0 3.3 collective-permute-done.4
  218.3 5.2 subtract_convert_fusion.2
  223.5 0.7 fusion.6
  224.3 2.7 fusion.39
  227.0 2.8 fusion.33
  229.8 5.2 collective-permute-done.5
  235.0 5.1 subtract_convert_fusion.1
  240.1 0.7 fusion.5
  240.9 0.3 collective-permute-start.6
  241.2 2.7 fusion.27
  243.8 2.8 fusion.21
  246.6 5.3 collective-permute-done.6
  251.9 5.2 subtract_convert_fusion
  257.1 2.7 fusion.15
  259.7 17.9 %scatter_custom_fusion.1 = bf16[4096,512]{1,0:T(8,128)(2,1)} fusion(s32[2048]{0:T(1024)} %bitcast.223, f32[2048,512]{1,0:T(8,128)} %fusion.15, f32[2048,512]{1,0:T(8,128)} %fusion.21, f32[2048,512]{1,0:T(8,128)} %fusion.27, f32[2048,512]{1,0:T(8,128)} %fusion.33, f32[2048,512]{1,0:T(8,128)} %fusion.39, f32[2048,512]{1,0:T(8,128)} %fusion.45, ...), kind=kCustom, calls=%fused_computation.8 | custom fusion | flops 8388608 | bytes 37749248 | tf_op jit(solution)/shard_map/scatter | solution.py:24
  277.6 9.1 %convert_bitcast_fusion = bf16[512,16,512]{0,2,1:T(8,128)(2,1)} fusion(bf16[16,256,512]{2,1,0:T(8,128)(2,1)} %bitcast.215, bf16[16,256,512]{2,1,0:T(8,128)(2,1)} %bitcast.214), kind=kOutput, calls=%fused_computation.4 | convolution fusion | flops 2151677952 | bytes 16777216 | tf_op jit(solution)/shard_map/kmd,kme->dke/dot_general | solution.py:69
  286.8 0.3 all-reduce.3.cloned.1.call-start
  287.1 0.3 copy-done.71
  287.4 0.6 dynamic-slice
  288.7 116.0 %reduce-scatter.2.cloned.1.call-done = bf16[512,2,512]{0,2,1:T(8,128)(2,1)} async-done(((bf16[512,16,512]{0,2,1:T(8,128)(2,1)}), bf16[512,2,512]{0,2,1:T(8,128)(2,1)}) %reduce-scatter.2.cloned.1.call-update) | async-done | bytes 1048592 | tf_op jit(solution)/shard_map/reduce_scatter | solution.py:70
  404.7 3.7 copy.14
  408.4 9.2 %convolution_convert_fusion = bf16[16,256,512]{2,1,0:T(8,128)(2,1)} fusion(bf16[16,256,512]{2,1,0:T(8,128)(2,1)} %bitcast.216, bf16[16,512,512]{2,1,0:T(8,128)(2,1)} %all-gather.2.cloned.1.call-done), kind=kOutput, calls=%fused_computation.6 | convolution fusion | flops 2149580800 | bytes 16777216 | tf_op jit(solution)/shard_map/kme,kde->kmd/dot_general | solution.py:66
  417.6 12.0 %gather_fusion.1 = bf16[2048,512]{1,0:T(8,128)(2,1)} fusion(bf16[4096,512]{1,0:T(8,128)(2,1)} %bitcast.212, s32[2048]{0:T(1024)S(1)} %copy-done.4), kind=kCustom, calls=%fused_computation.1 | custom fusion | bytes 4202496 | tf_op jit(solution)/shard_map/gather | solution.py:73
  429.6 2.6 fusion.4
  432.1 95.1 %all-reduce.3.cloned.1.call-done = bf16[512,2,512]{2,1,0:T(2,128)(2,1)} async-done(((bf16[512,2,512]{2,1,0:T(2,128)(2,1)}), bf16[512,2,512]{2,1,0:T(2,128)(2,1)}) %all-reduce.3.cloned.1.call-update) | async-done | bytes 1048592
  527.3 1.5 dynamic-slice_convert_fusion
  (165 shorter events, 1.2 us)
Async XLA Ops:
  7.2 114.1 %all-gather.2.cloned.1.call-start = ((), (), s32[]{:S(2)}) async-start(), calls=%async_computation.1 | async-start | bytes 9437184 | tf_op jit(solution)/shard_map/all_gather | solution.py:35
  7.9 396.8 %reduce-scatter.2.cloned.1.call-start = ((), (), s32[]{:S(2)}) async-start(), calls=%async_computation.2 | async-start | bytes 9437184 | tf_op jit(solution)/shard_map/reduce_scatter | solution.py:70
  15.4 13.8 %copy-start.5 = (s32[2048,1]{0,1:T(1,128)}, s32[2048,1]{0,1:T(1,128)S(1)}, u32[]{:S(2)}) copy-start(s32[2048,1]{0,1:T(1,128)S(1)} %compare_select_fusion) | copy-start | bytes 24580
  15.4 13.8 %copy-start = (s32[8,2048,16]{1,2,0:T(8,128)S(1)}, s32[8,2048,16]{1,2,0:T(8,128)}, u32[]{:S(2)}) copy-start(s32[8,2048,16]{1,2,0:T(8,128)} %param.11) | copy-start | bytes 3145732
  29.2 101.2 %copy-start.3 = (s32[2048]{0:T(1024)}, s32[2048]{0:T(1024)S(1)}, u32[]{:S(2)}) copy-start(s32[2048]{0:T(1024)S(1)} %broadcast_clamp_fusion) | copy-start | bytes 24580
  130.4 10.4 %copy-start.1 = (f32[256,512]{1,0:T(8,128)S(1)}, f32[256,512]{1,0:T(8,128)}, u32[]{:S(2)}) copy-start(f32[256,512]{1,0:T(8,128)} %param.9) | copy-start | bytes 1572868
  130.4 10.4 %copy-start.69 = (s32[2048]{0:T(1024)S(1)}, s32[2048]{0:T(1024)}, u32[]{:S(2)}) copy-start(s32[2048]{0:T(1024)} %param.10) | copy-start | bytes 24580
  146.0 10.1 %copy-start.53 = (s32[2048,1]{0,1:T(1,128)S(1)}, s32[2048,1]{0,1:T(1,128)}, u32[]{:S(2)}) copy-start(s32[2048,1]{0,1:T(1,128)} %get-tuple-element.113) | copy-start | bytes 24580
  146.0 10.1 %copy-start.54 = (s32[2048,1]{0,1:T(1,128)S(1)}, s32[2048,1]{0,1:T(1,128)}, u32[]{:S(2)}) copy-start(s32[2048,1]{0,1:T(1,128)} %get-tuple-element.114) | copy-start | bytes 24580
  146.1 10.1 %copy-start.55 = (s32[2048,1]{0,1:T(1,128)S(1)}, s32[2048,1]{0,1:T(1,128)}, u32[]{:S(2)}) copy-start(s32[2048,1]{0,1:T(1,128)} %get-tuple-element.115) | copy-start | bytes 24580
  146.1 10.1 %copy-start.56 = (s32[2048,1]{0,1:T(1,128)S(1)}, s32[2048,1]{0,1:T(1,128)}, u32[]{:S(2)}) copy-start(s32[2048,1]{0,1:T(1,128)} %get-tuple-element.116) | copy-start | bytes 24580
  146.1 10.1 %copy-start.57 = (s32[2048,1]{0,1:T(1,128)S(1)}, s32[2048,1]{0,1:T(1,128)}, u32[]{:S(2)}) copy-start(s32[2048,1]{0,1:T(1,128)} %get-tuple-element.117) | copy-start | bytes 24580
  146.1 10.1 %copy-start.58 = (s32[2048,1]{0,1:T(1,128)S(1)}, s32[2048,1]{0,1:T(1,128)}, u32[]{:S(2)}) copy-start(s32[2048,1]{0,1:T(1,128)} %get-tuple-element.118) | copy-start | bytes 24580
  146.1 10.1 %copy-start.59 = (s32[2048,1]{0,1:T(1,128)S(1)}, s32[2048,1]{0,1:T(1,128)}, u32[]{:S(2)}) copy-start(s32[2048,1]{0,1:T(1,128)} %get-tuple-element.119) | copy-start | bytes 24580
  146.1 10.1 %copy-start.60 = (s32[2048,1]{0,1:T(1,128)S(1)}, s32[2048,1]{0,1:T(1,128)}, u32[]{:S(2)}) copy-start(s32[2048,1]{0,1:T(1,128)} %get-tuple-element.120) | copy-start | bytes 24580
  146.1 10.1 %copy-start.61 = (s32[2048,1]{0,1:T(1,128)S(1)}, s32[2048,1]{0,1:T(1,128)}, u32[]{:S(2)}) copy-start(s32[2048,1]{0,1:T(1,128)} %get-tuple-element.121) | copy-start | bytes 24580
  146.1 10.1 %copy-start.62 = (s32[2048,1]{0,1:T(1,128)S(1)}, s32[2048,1]{0,1:T(1,128)}, u32[]{:S(2)}) copy-start(s32[2048,1]{0,1:T(1,128)} %get-tuple-element.122) | copy-start | bytes 24580
  146.1 10.1 %copy-start.63 = (s32[2048,1]{0,1:T(1,128)S(1)}, s32[2048,1]{0,1:T(1,128)}, u32[]{:S(2)}) copy-start(s32[2048,1]{0,1:T(1,128)} %get-tuple-element.123) | copy-start | bytes 24580
  146.1 10.1 %copy-start.64 = (s32[2048,1]{0,1:T(1,128)S(1)}, s32[2048,1]{0,1:T(1,128)}, u32[]{:S(2)}) copy-start(s32[2048,1]{0,1:T(1,128)} %get-tuple-element.124) | copy-start | bytes 24580
  146.2 10.1 %copy-start.65 = (s32[2048,1]{0,1:T(1,128)S(1)}, s32[2048,1]{0,1:T(1,128)}, u32[]{:S(2)}) copy-start(s32[2048,1]{0,1:T(1,128)} %get-tuple-element.125) | copy-start | bytes 24580
  146.2 10.1 %copy-start.66 = (s32[2048,1]{0,1:T(1,128)S(1)}, s32[2048,1]{0,1:T(1,128)}, u32[]{:S(2)}) copy-start(s32[2048,1]{0,1:T(1,128)} %get-tuple-element.126) | copy-start | bytes 24580
  146.2 10.1 %copy-start.67 = (s32[2048,1]{0,1:T(1,128)S(1)}, s32[2048,1]{0,1:T(1,128)}, u32[]{:S(2)}) copy-start(s32[2048,1]{0,1:T(1,128)} %get-tuple-element.127) | copy-start | bytes 24580
  146.2 10.1 %copy-start.68 = (s32[2048,1]{0,1:T(1,128)S(1)}, s32[2048,1]{0,1:T(1,128)}, u32[]{:S(2)}) copy-start(s32[2048,1]{0,1:T(1,128)} %get-tuple-element.128) | copy-start | bytes 24580
  146.2 10.1 %copy-start.70 = (s32[2048]{0:T(1024)S(1)}, s32[2048]{0:T(1024)}, u32[]{:S(2)}) copy-start(s32[2048]{0:T(1024)} %param.10) | copy-start | bytes 24580
  146.2 10.1 %copy-start.73 = (s32[256]{0:T(256)S(1)}, s32[256]{0:T(256)}, u32[]{:S(2)}) copy-start(s32[256]{0:T(256)} %iota_add_fusion.6) | copy-start | bytes 3076
  147.0 9.2 %collective-permute-start = (f32[256,512]{1,0:T(8,128)S(1)}, f32[256,512]{1,0:T(8,128)S(1)}, u32[]{:S(2)}, u32[]{:S(2)}) collective-permute-start(f32[256,512]{1,0:T(8,128)S(1)} %fusion.11), channel_id=1, source_target_pairs={{120,0},{0,8},{8,16},{16,24},{24,32},{32,40},{40,48},{48,56},{56,6... | collective-permute-start | bytes 1572872 | tf_op jit(solution)/shard_map/ppermute | solution.py:13
  161.5 9.6 %copy-start.37 = (s32[2048,1]{0,1:T(1,128)S(1)}, s32[2048,1]{0,1:T(1,128)}, u32[]{:S(2)}) copy-start(s32[2048,1]{0,1:T(1,128)} %get-tuple-element.97) | copy-start | bytes 24580
  161.5 9.6 %copy-start.38 = (s32[2048,1]{0,1:T(1,128)S(1)}, s32[2048,1]{0,1:T(1,128)}, u32[]{:S(2)}) copy-start(s32[2048,1]{0,1:T(1,128)} %get-tuple-element.98) | copy-start | bytes 24580
  161.5 9.6 %copy-start.39 = (s32[2048,1]{0,1:T(1,128)S(1)}, s32[2048,1]{0,1:T(1,128)}, u32[]{:S(2)}) copy-start(s32[2048,1]{0,1:T(1,128)} %get-tuple-element.99) | copy-start | bytes 24580
  161.5 9.6 %copy-start.40 = (s32[2048,1]{0,1:T(1,128)S(1)}, s32[2048,1]{0,1:T(1,128)}, u32[]{:S(2)}) copy-start(s32[2048,1]{0,1:T(1,128)} %get-tuple-element.100) | copy-start | bytes 24580
  161.6 9.6 %copy-start.41 = (s32[2048,1]{0,1:T(1,128)S(1)}, s32[2048,1]{0,1:T(1,128)}, u32[]{:S(2)}) copy-start(s32[2048,1]{0,1:T(1,128)} %get-tuple-element.101) | copy-start | bytes 24580
  161.6 9.6 %copy-start.42 = (s32[2048,1]{0,1:T(1,128)S(1)}, s32[2048,1]{0,1:T(1,128)}, u32[]{:S(2)}) copy-start(s32[2048,1]{0,1:T(1,128)} %get-tuple-element.102) | copy-start | bytes 24580
  161.6 9.6 %copy-start.43 = (s32[2048,1]{0,1:T(1,128)S(1)}, s32[2048,1]{0,1:T(1,128)}, u32[]{:S(2)}) copy-start(s32[2048,1]{0,1:T(1,128)} %get-tuple-element.103) | copy-start | bytes 24580
  161.6 9.6 %copy-start.44 = (s32[2048,1]{0,1:T(1,128)S(1)}, s32[2048,1]{0,1:T(1,128)}, u32[]{:S(2)}) copy-start(s32[2048,1]{0,1:T(1,128)} %get-tuple-element.104) | copy-start | bytes 24580
  161.6 9.6 %copy-start.45 = (s32[2048,1]{0,1:T(1,128)S(1)}, s32[2048,1]{0,1:T(1,128)}, u32[]{:S(2)}) copy-start(s32[2048,1]{0,1:T(1,128)} %get-tuple-element.105) | copy-start | bytes 24580
  161.6 9.6 %copy-start.46 = (s32[2048,1]{0,1:T(1,128)S(1)}, s32[2048,1]{0,1:T(1,128)}, u32[]{:S(2)}) copy-start(s32[2048,1]{0,1:T(1,128)} %get-tuple-element.106) | copy-start | bytes 24580
  161.6 9.6 %copy-start.47 = (s32[2048,1]{0,1:T(1,128)S(1)}, s32[2048,1]{0,1:T(1,128)}, u32[]{:S(2)}) copy-start(s32[2048,1]{0,1:T(1,128)} %get-tuple-element.107) | copy-start | bytes 24580
  161.6 9.6 %copy-start.48 = (s32[2048,1]{0,1:T(1,128)S(1)}, s32[2048,1]{0,1:T(1,128)}, u32[]{:S(2)}) copy-start(s32[2048,1]{0,1:T(1,128)} %get-tuple-element.108) | copy-start | bytes 24580
  161.6 9.6 %copy-start.49 = (s32[2048,1]{0,1:T(1,128)S(1)}, s32[2048,1]{0,1:T(1,128)}, u32[]{:S(2)}) copy-start(s32[2048,1]{0,1:T(1,128)} %get-tuple-element.109) | copy-start | bytes 24580
  161.6 9.6 %copy-start.50 = (s32[2048,1]{0,1:T(1,128)S(1)}, s32[2048,1]{0,1:T(1,128)}, u32[]{:S(2)}) copy-start(s32[2048,1]{0,1:T(1,128)} %get-tuple-element.110) | copy-start | bytes 24580
  161.7 9.6 %copy-start.51 = (s32[2048,1]{0,1:T(1,128)S(1)}, s32[2048,1]{0,1:T(1,128)}, u32[]{:S(2)}) copy-start(s32[2048,1]{0,1:T(1,128)} %get-tuple-element.111) | copy-start | bytes 24580
  161.7 9.6 %copy-start.52 = (s32[2048,1]{0,1:T(1,128)S(1)}, s32[2048,1]{0,1:T(1,128)}, u32[]{:S(2)}) copy-start(s32[2048,1]{0,1:T(1,128)} %get-tuple-element.112) | copy-start | bytes 24580
  161.7 9.6 %copy-start.72 = (s32[256]{0:T(256)S(1)}, s32[256]{0:T(256)}, u32[]{:S(2)}) copy-start(s32[256]{0:T(256)} %iota_add_fusion.5) | copy-start | bytes 3076
  162.4 8.7 %collective-permute-start.1 = (f32[256,512]{1,0:T(8,128)S(1)}, f32[256,512]{1,0:T(8,128)S(1)}, u32[]{:S(2)}, u32[]{:S(2)}) collective-permute-start(f32[256,512]{1,0:T(8,128)S(1)} %fusion.10), channel_id=1, source_target_pairs={{120,0},{0,8},{8,16},{16,24},{24,32},{32,40},{40,48},{48,56},{56,6... | collective-permute-start | bytes 1572872 | tf_op jit(solution)/shard_map/ppermute | solution.py:13
  176.4 9.6 %copy-start.21 = (s32[2048,1]{0,1:T(1,128)S(1)}, s32[2048,1]{0,1:T(1,128)}, u32[]{:S(2)}) copy-start(s32[2048,1]{0,1:T(1,128)} %get-tuple-element.81) | copy-start | bytes 24580
  176.5 9.6 %copy-start.22 = (s32[2048,1]{0,1:T(1,128)S(1)}, s32[2048,1]{0,1:T(1,128)}, u32[]{:S(2)}) copy-start(s32[2048,1]{0,1:T(1,128)} %get-tuple-element.82) | copy-start | bytes 24580
  176.5 9.6 %copy-start.23 = (s32[2048,1]{0,1:T(1,128)S(1)}, s32[2048,1]{0,1:T(1,128)}, u32[]{:S(2)}) copy-start(s32[2048,1]{0,1:T(1,128)} %get-tuple-element.83) | copy-start | bytes 24580
  176.5 9.6 %copy-start.24 = (s32[2048,1]{0,1:T(1,128)S(1)}, s32[2048,1]{0,1:T(1,128)}, u32[]{:S(2)}) copy-start(s32[2048,1]{0,1:T(1,128)} %get-tuple-element.84) | copy-start | bytes 24580
  176.5 9.6 %copy-start.25 = (s32[2048,1]{0,1:T(1,128)S(1)}, s32[2048,1]{0,1:T(1,128)}, u32[]{:S(2)}) copy-start(s32[2048,1]{0,1:T(1,128)} %get-tuple-element.85) | copy-start | bytes 24580
  176.5 9.6 %copy-start.26 = (s32[2048,1]{0,1:T(1,128)S(1)}, s32[2048,1]{0,1:T(1,128)}, u32[]{:S(2)}) copy-start(s32[2048,1]{0,1:T(1,128)} %get-tuple-element.86) | copy-start | bytes 24580
  176.5 9.6 %copy-start.27 = (s32[2048,1]{0,1:T(1,128)S(1)}, s32[2048,1]{0,1:T(1,128)}, u32[]{:S(2)}) copy-start(s32[2048,1]{0,1:T(1,128)} %get-tuple-element.87) | copy-start | bytes 24580
  176.5 9.6 %copy-start.28 = (s32[2048,1]{0,1:T(1,128)S(1)}, s32[2048,1]{0,1:T(1,128)}, u32[]{:S(2)}) copy-start(s32[2048,1]{0,1:T(1,128)} %get-tuple-element.88) | copy-start | bytes 24580
  176.5 9.6 %copy-start.29 = (s32[2048,1]{0,1:T(1,128)S(1)}, s32[2048,1]{0,1:T(1,128)}, u32[]{:S(2)}) copy-start(s32[2048,1]{0,1:T(1,128)} %get-tuple-element.89) | copy-start | bytes 24580
  176.5 9.6 %copy-start.30 = (s32[2048,1]{0,1:T(1,128)S(1)}, s32[2048,1]{0,1:T(1,128)}, u32[]{:S(2)}) copy-start(s32[2048,1]{0,1:T(1,128)} %get-tuple-element.90) | copy-start | bytes 24580
  176.5 9.6 %copy-start.31 = (s32[2048,1]{0,1:T(1,128)S(1)}, s32[2048,1]{0,1:T(1,128)}, u32[]{:S(2)}) copy-start(s32[2048,1]{0,1:T(1,128)} %get-tuple-element.91) | copy-start | bytes 24580
  176.6 9.6 %copy-start.32 = (s32[2048,1]{0,1:T(1,128)S(1)}, s32[2048,1]{0,1:T(1,128)}, u32[]{:S(2)}) copy-start(s32[2048,1]{0,1:T(1,128)} %get-tuple-element.92) | copy-start | bytes 24580
  176.6 9.6 %copy-start.33 = (s32[2048,1]{0,1:T(1,128)S(1)}, s32[2048,1]{0,1:T(1,128)}, u32[]{:S(2)}) copy-start(s32[2048,1]{0,1:T(1,128)} %get-tuple-element.93) | copy-start | bytes 24580
  176.6 9.6 %copy-start.34 = (s32[2048,1]{0,1:T(1,128)S(1)}, s32[2048,1]{0,1:T(1,128)}, u32[]{:S(2)}) copy-start(s32[2048,1]{0,1:T(1,128)} %get-tuple-element.94) | copy-start | bytes 24580
  177.3 8.7 %collective-permute-start.2 = (f32[256,512]{1,0:T(8,128)S(1)}, f32[256,512]{1,0:T(8,128)S(1)}, u32[]{:S(2)}, u32[]{:S(2)}) collective-permute-start(f32[256,512]{1,0:T(8,128)S(1)} %fusion.9), channel_id=1, source_target_pairs={{120,0},{0,8},{8,16},{16,24},{24,32},{32,40},{40,48},{48,56},{56,6... | collective-permute-start | bytes 1572872 | tf_op jit(solution)/shard_map/ppermute | solution.py:13
  192.1 9.2 %collective-permute-start.3 = (f32[256,512]{1,0:T(8,128)S(1)}, f32[256,512]{1,0:T(8,128)S(1)}, u32[]{:S(2)}, u32[]{:S(2)}) collective-permute-start(f32[256,512]{1,0:T(8,128)S(1)} %fusion.8), channel_id=1, source_target_pairs={{120,0},{0,8},{8,16},{16,24},{24,32},{32,40},{40,48},{48,56},{56,6... | collective-permute-start | bytes 1572872 | tf_op jit(solution)/shard_map/ppermute | solution.py:13
  207.3 11.0 %collective-permute-start.4 = (f32[256,512]{1,0:T(8,128)S(1)}, f32[256,512]{1,0:T(8,128)S(1)}, u32[]{:S(2)}, u32[]{:S(2)}) collective-permute-start(f32[256,512]{1,0:T(8,128)S(1)} %fusion.7), channel_id=1, source_target_pairs={{120,0},{0,8},{8,16},{16,24},{24,32},{32,40},{40,48},{48,56},{56,6... | collective-permute-start | bytes 1572872 | tf_op jit(solution)/shard_map/ppermute | solution.py:13
  224.2 10.8 %collective-permute-start.5 = (f32[256,512]{1,0:T(8,128)S(1)}, f32[256,512]{1,0:T(8,128)S(1)}, u32[]{:S(2)}, u32[]{:S(2)}) collective-permute-start(f32[256,512]{1,0:T(8,128)S(1)} %fusion.6), channel_id=1, source_target_pairs={{120,0},{0,8},{8,16},{16,24},{24,32},{32,40},{40,48},{48,56},{56,6... | collective-permute-start | bytes 1572872 | tf_op jit(solution)/shard_map/ppermute | solution.py:13
  240.9 11.0 %collective-permute-start.6 = (f32[256,512]{1,0:T(8,128)S(1)}, f32[256,512]{1,0:T(8,128)S(1)}, u32[]{:S(2)}, u32[]{:S(2)}) collective-permute-start(f32[256,512]{1,0:T(8,128)S(1)} %fusion.5), channel_id=1, source_target_pairs={{120,0},{0,8},{8,16},{16,24},{24,32},{32,40},{40,48},{48,56},{56,6... | collective-permute-start | bytes 1572872 | tf_op jit(solution)/shard_map/ppermute | solution.py:13
  286.8 240.4 %all-reduce.3.cloned.1.call-start = ((), (), s32[]{:S(2)}) async-start(), calls=%async_computation.3 | async-start | bytes 2097152
  (20 other events, 133.6 us)
Sparse Core Ops, SparseCore 0:
  10.3 110.8 all-gather.1
  286.9 117.7 reduce-scatter.1
  408.5 118.7 all-reduce.2
where the time goes:
time: 544 us; the launch traced here: 536 us
  waiting for transfers between devices  336 us (62%)
  matrix products  98.4 us (18%)
  local copies, waits for them, and re-layouts  43.7 us (8%)
  other arithmetic  27.7 us (5%)
  between operations  15.9 us (3%)
  starting transfers between devices  13.7 us (3%)
    reduce_scatter x1, waiting for transfers between devices, shards(): lax.psum_scatter(terms.astype(jnp.bfloat16), 'rel', scatter_dimension=1,...  116 us
    unnamed x4, waiting for transfers between devices  95.8 us
    all_gather x1, waiting for transfers between devices, shards(): every_matrix = lax.all_gather(relations, 'rel', axis=0, tiled=True)  88.9 us
    dot_general x8, matrix products, shards(): lax.dot_general(queries, wide, (((1,), (1,)), ((), ())), preferred_elemen...  41.4 us
    ppermute x7, waiting for transfers between devices, from_behind(): return lax.ppermute(block, axis, route)  35.6 us
    dot_general x8, matrix products, shards(): jnp.dot(weight, wide, preferred_element_type=jnp.float32)  21.8 us
    scatter x1, other arithmetic, place_rows(): return jnp.zeros((total, rows.shape[1]), rows.dtype).at[slot].set(rows)  17.9 us
    ppermute x7, starting transfers between devices, from_behind(): return lax.ppermute(block, axis, route)  13.3 us
  transfers between devices with their start and end apart: 10, of which 10 were waited for; matrix products, arithmetic and copies ran while one was open for 13% of the time, Pallas kernels for 0%

commit v1 on v0

--- a/solution.py
+++ b/solution.py
@@ -32,7 +32,9 @@
     most = 2 * src_rows // nrel
     slot = slot_index(rel_ids, nrel, most)
     sent = place_rows(source_rows, slot, nrel * most).reshape(nrel, most, width)
-    every_matrix = lax.all_gather(relations, "rel", axis=0, tiled=True)
+    every_matrix = jnp.concatenate(
+        lax.all_to_all(jnp.stack([relations] * lax.axis_size("rel"), axis=0), "rel", 0, 0), axis=0
+    )
     q_slots = jnp.einsum(
         "kmd,kde->kme", sent, every_matrix, preferred_element_type=jnp.float32
     ).astype(jnp.bfloat16)

time: 544 us -> 571 us (1.050)
  waiting for transfers between devices: 336 us -> 352 us
  starting transfers between devices: 13.7 us -> 21.3 us
    all_gather x1 -> x0, waiting for transfers between devices: 88.9 us -> none  [shards(): every_matrix = lax.all_gather(relations, 'rel', axis=0, tiled=True)]
    all_to_all x0 -> x1, waiting for transfers between devices: none -> 73.7 us  [shards(): lax.all_to_all(jnp.stack([relations] * lax.axis_size('rel'), axis=0), 're...]
    reduce_scatter x1, waiting for transfers between devices: 116 us -> 148 us  [shards(): lax.psum_scatter(terms.astype(jnp.bfloat16), 'rel', scatter_dimension=1,...]
    all_to_all x0 -> x1, starting transfers between devices: none -> 8.28 us  [shards(): lax.all_to_all(jnp.stack([relations] * lax.axis_size('rel'), axis=0), 're...]
    unnamed x4 -> x3, waiting for transfers between devices: 95.8 us -> 95 us
  transfers between devices with their start and end apart: 10 -> 10, of which waited for: 10 -> 10; matrix products, arithmetic and copies ran while one was open for 13% -> 12% of each run, Pallas kernels for 0% -> 0%
where the time goes in v1:
time: 571 us; the launch traced here: 563 us
  waiting for transfers between devices  352 us (62%)
  matrix products  98.4 us (17%)
  local copies, waits for them, and re-layouts  49 us (9%)
  other arithmetic  25.5 us (4%)
  starting transfers between devices  21.3 us (4%)
  between operations  16.4 us (3%)
    reduce_scatter x1, waiting for transfers between devices, shards(): lax.psum_scatter(terms.astype(jnp.bfloat16), 'rel', scatter_dimension=1,...  148 us
    unnamed x3, waiting for transfers between devices  95 us
    all_to_all x1, waiting for transfers between devices, shards(): lax.all_to_all(jnp.stack([relations] * lax.axis_size('rel'), axis=0), 're...  73.7 us
    dot_general x8, matrix products, shards(): lax.dot_general(queries, wide, (((1,), (1,)), ((), ())), preferred_elemen...  41.4 us
    ppermute x7, waiting for transfers between devices, from_behind(): return lax.ppermute(block, axis, route)  35.4 us
    dot_general x8, matrix products, shards(): jnp.dot(weight, wide, preferred_element_type=jnp.float32)  21.8 us
    scatter x1, other arithmetic, place_rows(): return jnp.zeros((total, rows.shape[1]), rows.dtype).at[slot].set(rows)  17.9 us
    ppermute x7, starting transfers between devices, from_behind(): return lax.ppermute(block, axis, route)  12.6 us
  transfers between devices with their start and end apart: 10, of which 10 were waited for; matrix products, arithmetic and copies ran while one was open for 12% of the time, Pallas kernels for 0%

profile of v1, /device:TPU:1, one launch (start us, length us, event | category | flops | bytes accessed | tf_op | source)
XLA Modules:
  0.0 562.6 jit_solution(3673270064968379309)
XLA Ops:
  7.2 5.3 stack.2
  12.5 8.3 %all-to-all-start = ((bf16[8,2,512,512]{3,2,1,0:T(8,128)(2,1)}), bf16[8,2,512,512]{3,2,1,0:T(8,128)(2,1)}, u32[]{:S(2)}, u32[]{:S(2)}) async-start(bf16[8,2,512,512]{3,2,1,0:T(8,128)(2,1)} %stack.2), calls=%async_computation | async-start | bytes 16777216 | tf_op jit(solution)/shard_map/all_to_all | solution.py:36
  20.9 4.5 reduce-window.6
  25.4 0.4 slice_reduce_fusion
  25.8 0.2 reduce-window.9
  26.0 0.1 broadcast_add_fusion
  26.2 12.6 %scatter_custom_fusion = bf16[4096,512]{1,0:T(8,128)(2,1)} fusion(s32[2048]{0:T(1024)S(1)} %bitcast.222, bf16[2048,512]{1,0:T(8,128)(2,1)} %param.6, bf16[]{:T(256)} %constant.14.clone.1), kind=kCustom, calls=%fused_computation.131 | custom fusion | bytes 4194816 | tf_op jit(solution)/shard_map/scatter | solution.py:24
  38.9 0.5 iota_add_fusion.6
  39.4 0.6 iota_add_fusion.5
  40.2 0.7 fusion.70
  40.9 0.8 fusion.69
  41.7 0.7 fusion.68
  42.4 0.7 fusion.67
  43.2 73.7 %all-to-all-done = bf16[8,2,512,512]{3,2,1,0:T(8,128)(2,1)} async-done(((bf16[8,2,512,512]{3,2,1,0:T(8,128)(2,1)}), bf16[8,2,512,512]{3,2,1,0:T(8,128)(2,1)}, u32[]{:S(2)}, u32[]{:S(2)}) %all-to-all-start) | async-done | bytes 8388640 | tf_op jit(solution)/shard_map/all_to_all | solution.py:36
  116.9 9.2 %convolution_convert_fusion.1 = bf16[16,256,512]{2,1,0:T(8,128)(2,1)} fusion(bf16[16,256,512]{2,1,0:T(8,128)(2,1)} %bitcast.214, bf16[16,512,512]{2,1,0:T(8,128)(2,1)} %bitcast.23), kind=kOutput, calls=%fused_computation.7 | convolution fusion | flops 2149580800 | bytes 16777216 | tf_op jit(solution)/shard_map/kmd,kde->kme/dot_general | solution.py:38
  126.1 10.4 %gather_fusion = bf16[2048,512]{1,0:T(8,128)(2,1)S(1)} fusion(bf16[4096,512]{1,0:T(8,128)(2,1)} %bitcast.212, s32[2048]{0:T(1024)S(1)} %broadcast_clamp_fusion), kind=kCustom, calls=%fused_computation | custom fusion | bytes 4202496 | tf_op jit(solution)/shard_map/gather | solution.py:41
  136.5 5.2 subtract_convert_fusion.7
  141.9 0.7 fusion.11
  142.6 2.2 collective-permute-start
  144.9 6.0 %collective-permute-done = f32[256,512]{1,0:T(8,128)S(1)} collective-permute-done((f32[256,512]{1,0:T(8,128)S(1)}, f32[256,512]{1,0:T(8,128)S(1)}, u32[]{:S(2)}, u32[]{:S(2)}) %collective-permute-start) | collective-permute-done | bytes 524320 | tf_op jit(solution)/shard_map/ppermute | solution.py:13
  151.1 5.2 subtract_convert_fusion.6
  156.5 0.7 fusion.10
  157.2 2.6 collective-permute-start.1
  159.9 6.0 %collective-permute-done.1 = f32[256,512]{1,0:T(8,128)S(1)} collective-permute-done((f32[256,512]{1,0:T(8,128)S(1)}, f32[256,512]{1,0:T(8,128)S(1)}, u32[]{:S(2)}, u32[]{:S(2)}) %collective-permute-start.1) | collective-permute-done | bytes 524320 | tf_op jit(solution)/shard_map/ppermute | solution.py:13
  166.0 5.2 subtract_convert_fusion.5
  171.4 0.7 fusion.9
  172.1 2.6 collective-permute-start.2
  174.8 6.0 %collective-permute-done.2 = f32[256,512]{1,0:T(8,128)S(1)} collective-permute-done((f32[256,512]{1,0:T(8,128)S(1)}, f32[256,512]{1,0:T(8,128)S(1)}, u32[]{:S(2)}, u32[]{:S(2)}) %collective-permute-start.2) | collective-permute-done | bytes 524320 | tf_op jit(solution)/shard_map/ppermute | solution.py:13
  180.9 5.2 subtract_convert_fusion.4
  186.1 0.7 fusion.8
  186.9 2.6 collective-permute-start.3
  189.6 2.8 fusion.57
  192.4 3.6 collective-permute-done.3
  196.1 5.2 subtract_convert_fusion.3
  201.3 0.7 fusion.7
  202.0 2.3 collective-permute-start.4
  204.4 2.7 fusion.51
  207.0 2.8 fusion.45
  209.8 3.2 collective-permute-done.4
  213.0 5.2 subtract_convert_fusion.2
  218.2 0.7 fusion.6
  219.0 2.7 fusion.39
  221.7 2.8 fusion.33
  224.5 5.2 collective-permute-done.5
  229.7 5.1 subtract_convert_fusion.1
  234.9 0.7 fusion.5
  235.6 0.3 collective-permute-start.6
  236.0 2.6 fusion.27
  238.6 2.8 fusion.21
  241.4 5.3 collective-permute-done.6
  246.7 5.2 subtract_convert_fusion
  251.8 2.7 fusion.15
  254.5 17.9 %scatter_custom_fusion.1 = bf16[4096,512]{1,0:T(8,128)(2,1)} fusion(s32[2048]{0:T(1024)} %bitcast.224, f32[2048,512]{1,0:T(8,128)} %fusion.15, f32[2048,512]{1,0:T(8,128)} %fusion.21, f32[2048,512]{1,0:T(8,128)} %fusion.27, f32[2048,512]{1,0:T(8,128)} %fusion.33, f32[2048,512]{1,0:T(8,128)} %fusion.39, f32[2048,512]{1,0:T(8,128)} %fusion.45, ...), kind=kCustom, calls=%fused_computation.8 | custom fusion | flops 8388608 | bytes 37749248 | tf_op jit(solution)/shard_map/scatter | solution.py:24
  272.4 9.1 %convert_bitcast_fusion = bf16[512,16,512]{0,2,1:T(8,128)(2,1)} fusion(bf16[16,256,512]{2,1,0:T(8,128)(2,1)} %bitcast.216, bf16[16,256,512]{2,1,0:T(8,128)(2,1)} %bitcast.215), kind=kOutput, calls=%fused_computation.4 | convolution fusion | flops 2151677952 | bytes 16777216 | tf_op jit(solution)/shard_map/kmd,kme->dke/dot_general | solution.py:71
  281.6 0.3 all-reduce.3.cloned.1.call-start
  281.9 0.3 copy-done.72
  282.2 0.6 dynamic-slice
  283.5 147.9 %reduce-scatter.2.cloned.1.call-done = bf16[512,2,512]{0,2,1:T(8,128)(2,1)} async-done(((bf16[512,16,512]{0,2,1:T(8,128)(2,1)}), bf16[512,2,512]{0,2,1:T(8,128)(2,1)}) %reduce-scatter.2.cloned.1.call-update) | async-done | bytes 1048592 | tf_op jit(solution)/shard_map/reduce_scatter | solution.py:72
  431.4 3.7 copy.14
  435.1 9.2 %convolution_convert_fusion = bf16[16,256,512]{2,1,0:T(8,128)(2,1)} fusion(bf16[16,256,512]{2,1,0:T(8,128)(2,1)} %bitcast.217, bf16[16,512,512]{2,1,0:T(8,128)(2,1)} %bitcast.23), kind=kOutput, calls=%fused_computation.6 | convolution fusion | flops 2149580800 | bytes 16777216 | tf_op jit(solution)/shard_map/kme,kde->kmd/dot_general | solution.py:68
  444.3 12.0 %gather_fusion.1 = bf16[2048,512]{1,0:T(8,128)(2,1)} fusion(bf16[4096,512]{1,0:T(8,128)(2,1)} %bitcast.213, s32[2048]{0:T(1024)S(1)} %copy-done.4), kind=kCustom, calls=%fused_computation.1 | custom fusion | bytes 4202496 | tf_op jit(solution)/shard_map/gather | solution.py:75
  456.3 2.6 fusion.4
  458.8 94.9 %all-reduce.3.cloned.1.call-done = bf16[512,2,512]{2,1,0:T(2,128)(2,1)} async-done(((bf16[512,2,512]{2,1,0:T(2,128)(2,1)}), bf16[512,2,512]{2,1,0:T(2,128)(2,1)}) %all-reduce.3.cloned.1.call-update) | async-done | bytes 1048592
  553.7 1.5 dynamic-slice_convert_fusion
  (167 shorter events, 1.0 us)
Async XLA Ops:
  12.5 104.4 %all-to-all-start = ((bf16[8,2,512,512]{3,2,1,0:T(8,128)(2,1)}), bf16[8,2,512,512]{3,2,1,0:T(8,128)(2,1)}, u32[]{:S(2)}, u32[]{:S(2)}) async-start(bf16[8,2,512,512]{3,2,1,0:T(8,128)(2,1)} %stack.2), calls=%async_computation | async-start | bytes 16777216 | tf_op jit(solution)/shard_map/all_to_all | solution.py:36
  20.8 410.6 %reduce-scatter.2.cloned.1.call-start = ((), (), s32[]{:S(2)}) async-start(), calls=%async_computation.2 | async-start | bytes 9437184 | tf_op jit(solution)/shard_map/reduce_scatter | solution.py:72
  26.2 13.7 %copy-start.6 = (s32[2048,1]{0,1:T(1,128)}, s32[2048,1]{0,1:T(1,128)S(1)}, u32[]{:S(2)}) copy-start(s32[2048,1]{0,1:T(1,128)S(1)} %compare_select_fusion) | copy-start | bytes 24580
  26.2 13.7 %copy-start = (s32[8,2048,16]{1,2,0:T(8,128)S(1)}, s32[8,2048,16]{1,2,0:T(8,128)}, u32[]{:S(2)}) copy-start(s32[8,2048,16]{1,2,0:T(8,128)} %param.11) | copy-start | bytes 3145732
  40.0 86.1 %copy-start.3 = (s32[2048]{0:T(1024)}, s32[2048]{0:T(1024)S(1)}, u32[]{:S(2)}) copy-start(s32[2048]{0:T(1024)S(1)} %broadcast_clamp_fusion) | copy-start | bytes 24580
  126.1 10.4 %copy-start.1 = (f32[256,512]{1,0:T(8,128)S(1)}, f32[256,512]{1,0:T(8,128)}, u32[]{:S(2)}) copy-start(f32[256,512]{1,0:T(8,128)} %param.9) | copy-start | bytes 1572868
  126.1 10.4 %copy-start.70 = (s32[2048]{0:T(1024)S(1)}, s32[2048]{0:T(1024)}, u32[]{:S(2)}) copy-start(s32[2048]{0:T(1024)} %param.10) | copy-start | bytes 24580
  141.7 9.3 %copy-start.54 = (s32[2048,1]{0,1:T(1,128)S(1)}, s32[2048,1]{0,1:T(1,128)}, u32[]{:S(2)}) copy-start(s32[2048,1]{0,1:T(1,128)} %get-tuple-element.113) | copy-start | bytes 24580
  141.7 9.3 %copy-start.55 = (s32[2048,1]{0,1:T(1,128)S(1)}, s32[2048,1]{0,1:T(1,128)}, u32[]{:S(2)}) copy-start(s32[2048,1]{0,1:T(1,128)} %get-tuple-element.114) | copy-start | bytes 24580
  141.7 9.2 %copy-start.56 = (s32[2048,1]{0,1:T(1,128)S(1)}, s32[2048,1]{0,1:T(1,128)}, u32[]{:S(2)}) copy-start(s32[2048,1]{0,1:T(1,128)} %get-tuple-element.115) | copy-start | bytes 24580
  141.7 9.2 %copy-start.57 = (s32[2048,1]{0,1:T(1,128)S(1)}, s32[2048,1]{0,1:T(1,128)}, u32[]{:S(2)}) copy-start(s32[2048,1]{0,1:T(1,128)} %get-tuple-element.116) | copy-start | bytes 24580
  141.7 9.2 %copy-start.58 = (s32[2048,1]{0,1:T(1,128)S(1)}, s32[2048,1]{0,1:T(1,128)}, u32[]{:S(2)}) copy-start(s32[2048,1]{0,1:T(1,128)} %get-tuple-element.117) | copy-start | bytes 24580
  141.7 9.2 %copy-start.59 = (s32[2048,1]{0,1:T(1,128)S(1)}, s32[2048,1]{0,1:T(1,128)}, u32[]{:S(2)}) copy-start(s32[2048,1]{0,1:T(1,128)} %get-tuple-element.118) | copy-start | bytes 24580
  141.8 9.2 %copy-start.60 = (s32[2048,1]{0,1:T(1,128)S(1)}, s32[2048,1]{0,1:T(1,128)}, u32[]{:S(2)}) copy-start(s32[2048,1]{0,1:T(1,128)} %get-tuple-element.119) | copy-start | bytes 24580
  141.8 9.2 %copy-start.61 = (s32[2048,1]{0,1:T(1,128)S(1)}, s32[2048,1]{0,1:T(1,128)}, u32[]{:S(2)}) copy-start(s32[2048,1]{0,1:T(1,128)} %get-tuple-element.120) | copy-start | bytes 24580
  141.8 9.2 %copy-start.62 = (s32[2048,1]{0,1:T(1,128)S(1)}, s32[2048,1]{0,1:T(1,128)}, u32[]{:S(2)}) copy-start(s32[2048,1]{0,1:T(1,128)} %get-tuple-element.121) | copy-start | bytes 24580
  141.8 9.2 %copy-start.63 = (s32[2048,1]{0,1:T(1,128)S(1)}, s32[2048,1]{0,1:T(1,128)}, u32[]{:S(2)}) copy-start(s32[2048,1]{0,1:T(1,128)} %get-tuple-element.122) | copy-start | bytes 24580
  141.8 9.2 %copy-start.64 = (s32[2048,1]{0,1:T(1,128)S(1)}, s32[2048,1]{0,1:T(1,128)}, u32[]{:S(2)}) copy-start(s32[2048,1]{0,1:T(1,128)} %get-tuple-element.123) | copy-start | bytes 24580
  141.8 9.2 %copy-start.65 = (s32[2048,1]{0,1:T(1,128)S(1)}, s32[2048,1]{0,1:T(1,128)}, u32[]{:S(2)}) copy-start(s32[2048,1]{0,1:T(1,128)} %get-tuple-element.124) | copy-start | bytes 24580
  141.8 9.2 %copy-start.66 = (s32[2048,1]{0,1:T(1,128)S(1)}, s32[2048,1]{0,1:T(1,128)}, u32[]{:S(2)}) copy-start(s32[2048,1]{0,1:T(1,128)} %get-tuple-element.125) | copy-start | bytes 24580
  141.8 9.2 %copy-start.67 = (s32[2048,1]{0,1:T(1,128)S(1)}, s32[2048,1]{0,1:T(1,128)}, u32[]{:S(2)}) copy-start(s32[2048,1]{0,1:T(1,128)} %get-tuple-element.126) | copy-start | bytes 24580
  141.8 9.2 %copy-start.68 = (s32[2048,1]{0,1:T(1,128)S(1)}, s32[2048,1]{0,1:T(1,128)}, u32[]{:S(2)}) copy-start(s32[2048,1]{0,1:T(1,128)} %get-tuple-element.127) | copy-start | bytes 24580
  141.8 9.2 %copy-start.69 = (s32[2048,1]{0,1:T(1,128)S(1)}, s32[2048,1]{0,1:T(1,128)}, u32[]{:S(2)}) copy-start(s32[2048,1]{0,1:T(1,128)} %get-tuple-element.128) | copy-start | bytes 24580
  142.6 8.3 %collective-permute-start = (f32[256,512]{1,0:T(8,128)S(1)}, f32[256,512]{1,0:T(8,128)S(1)}, u32[]{:S(2)}, u32[]{:S(2)}) collective-permute-start(f32[256,512]{1,0:T(8,128)S(1)} %fusion.11), channel_id=1, source_target_pairs={{120,0},{0,8},{8,16},{16,24},{24,32},{32,40},{40,48},{48,56},{56,6... | collective-permute-start | bytes 1572872 | tf_op jit(solution)/shard_map/ppermute | solution.py:13
  156.3 9.6 %copy-start.38 = (s32[2048,1]{0,1:T(1,128)S(1)}, s32[2048,1]{0,1:T(1,128)}, u32[]{:S(2)}) copy-start(s32[2048,1]{0,1:T(1,128)} %get-tuple-element.97) | copy-start | bytes 24580
  156.3 9.6 %copy-start.39 = (s32[2048,1]{0,1:T(1,128)S(1)}, s32[2048,1]{0,1:T(1,128)}, u32[]{:S(2)}) copy-start(s32[2048,1]{0,1:T(1,128)} %get-tuple-element.98) | copy-start | bytes 24580
  156.3 9.6 %copy-start.40 = (s32[2048,1]{0,1:T(1,128)S(1)}, s32[2048,1]{0,1:T(1,128)}, u32[]{:S(2)}) copy-start(s32[2048,1]{0,1:T(1,128)} %get-tuple-element.99) | copy-start | bytes 24580
  156.3 9.6 %copy-start.41 = (s32[2048,1]{0,1:T(1,128)S(1)}, s32[2048,1]{0,1:T(1,128)}, u32[]{:S(2)}) copy-start(s32[2048,1]{0,1:T(1,128)} %get-tuple-element.100) | copy-start | bytes 24580
  156.3 9.6 %copy-start.42 = (s32[2048,1]{0,1:T(1,128)S(1)}, s32[2048,1]{0,1:T(1,128)}, u32[]{:S(2)}) copy-start(s32[2048,1]{0,1:T(1,128)} %get-tuple-element.101) | copy-start | bytes 24580
  156.4 9.6 %copy-start.43 = (s32[2048,1]{0,1:T(1,128)S(1)}, s32[2048,1]{0,1:T(1,128)}, u32[]{:S(2)}) copy-start(s32[2048,1]{0,1:T(1,128)} %get-tuple-element.102) | copy-start | bytes 24580
  156.4 9.6 %copy-start.44 = (s32[2048,1]{0,1:T(1,128)S(1)}, s32[2048,1]{0,1:T(1,128)}, u32[]{:S(2)}) copy-start(s32[2048,1]{0,1:T(1,128)} %get-tuple-element.103) | copy-start | bytes 24580
  156.4 9.6 %copy-start.45 = (s32[2048,1]{0,1:T(1,128)S(1)}, s32[2048,1]{0,1:T(1,128)}, u32[]{:S(2)}) copy-start(s32[2048,1]{0,1:T(1,128)} %get-tuple-element.104) | copy-start | bytes 24580
  156.4 9.6 %copy-start.46 = (s32[2048,1]{0,1:T(1,128)S(1)}, s32[2048,1]{0,1:T(1,128)}, u32[]{:S(2)}) copy-start(s32[2048,1]{0,1:T(1,128)} %get-tuple-element.105) | copy-start | bytes 24580
  156.4 9.6 %copy-start.47 = (s32[2048,1]{0,1:T(1,128)S(1)}, s32[2048,1]{0,1:T(1,128)}, u32[]{:S(2)}) copy-start(s32[2048,1]{0,1:T(1,128)} %get-tuple-element.106) | copy-start | bytes 24580
  156.4 9.6 %copy-start.48 = (s32[2048,1]{0,1:T(1,128)S(1)}, s32[2048,1]{0,1:T(1,128)}, u32[]{:S(2)}) copy-start(s32[2048,1]{0,1:T(1,128)} %get-tuple-element.107) | copy-start | bytes 24580
  156.4 9.6 %copy-start.49 = (s32[2048,1]{0,1:T(1,128)S(1)}, s32[2048,1]{0,1:T(1,128)}, u32[]{:S(2)}) copy-start(s32[2048,1]{0,1:T(1,128)} %get-tuple-element.108) | copy-start | bytes 24580
  156.4 9.6 %copy-start.50 = (s32[2048,1]{0,1:T(1,128)S(1)}, s32[2048,1]{0,1:T(1,128)}, u32[]{:S(2)}) copy-start(s32[2048,1]{0,1:T(1,128)} %get-tuple-element.109) | copy-start | bytes 24580
  156.4 9.6 %copy-start.51 = (s32[2048,1]{0,1:T(1,128)S(1)}, s32[2048,1]{0,1:T(1,128)}, u32[]{:S(2)}) copy-start(s32[2048,1]{0,1:T(1,128)} %get-tuple-element.110) | copy-start | bytes 24580
  156.4 9.6 %copy-start.52 = (s32[2048,1]{0,1:T(1,128)S(1)}, s32[2048,1]{0,1:T(1,128)}, u32[]{:S(2)}) copy-start(s32[2048,1]{0,1:T(1,128)} %get-tuple-element.111) | copy-start | bytes 24580
  156.5 9.6 %copy-start.53 = (s32[2048,1]{0,1:T(1,128)S(1)}, s32[2048,1]{0,1:T(1,128)}, u32[]{:S(2)}) copy-start(s32[2048,1]{0,1:T(1,128)} %get-tuple-element.112) | copy-start | bytes 24580
  156.5 9.6 %copy-start.73 = (s32[256]{0:T(256)S(1)}, s32[256]{0:T(256)}, u32[]{:S(2)}) copy-start(s32[256]{0:T(256)} %iota_add_fusion.5) | copy-start | bytes 3076
  157.2 8.7 %collective-permute-start.1 = (f32[256,512]{1,0:T(8,128)S(1)}, f32[256,512]{1,0:T(8,128)S(1)}, u32[]{:S(2)}, u32[]{:S(2)}) collective-permute-start(f32[256,512]{1,0:T(8,128)S(1)} %fusion.10), channel_id=1, source_target_pairs={{120,0},{0,8},{8,16},{16,24},{24,32},{32,40},{40,48},{48,56},{56,6... | collective-permute-start | bytes 1572872 | tf_op jit(solution)/shard_map/ppermute | solution.py:13
  171.2 9.6 %copy-start.22 = (s32[2048,1]{0,1:T(1,128)S(1)}, s32[2048,1]{0,1:T(1,128)}, u32[]{:S(2)}) copy-start(s32[2048,1]{0,1:T(1,128)} %get-tuple-element.81) | copy-start | bytes 24580
  171.2 9.6 %copy-start.23 = (s32[2048,1]{0,1:T(1,128)S(1)}, s32[2048,1]{0,1:T(1,128)}, u32[]{:S(2)}) copy-start(s32[2048,1]{0,1:T(1,128)} %get-tuple-element.82) | copy-start | bytes 24580
  171.3 9.6 %copy-start.24 = (s32[2048,1]{0,1:T(1,128)S(1)}, s32[2048,1]{0,1:T(1,128)}, u32[]{:S(2)}) copy-start(s32[2048,1]{0,1:T(1,128)} %get-tuple-element.83) | copy-start | bytes 24580
  171.3 9.6 %copy-start.25 = (s32[2048,1]{0,1:T(1,128)S(1)}, s32[2048,1]{0,1:T(1,128)}, u32[]{:S(2)}) copy-start(s32[2048,1]{0,1:T(1,128)} %get-tuple-element.84) | copy-start | bytes 24580
  171.3 9.6 %copy-start.26 = (s32[2048,1]{0,1:T(1,128)S(1)}, s32[2048,1]{0,1:T(1,128)}, u32[]{:S(2)}) copy-start(s32[2048,1]{0,1:T(1,128)} %get-tuple-element.85) | copy-start | bytes 24580
  171.3 9.6 %copy-start.27 = (s32[2048,1]{0,1:T(1,128)S(1)}, s32[2048,1]{0,1:T(1,128)}, u32[]{:S(2)}) copy-start(s32[2048,1]{0,1:T(1,128)} %get-tuple-element.86) | copy-start | bytes 24580
  171.3 9.6 %copy-start.28 = (s32[2048,1]{0,1:T(1,128)S(1)}, s32[2048,1]{0,1:T(1,128)}, u32[]{:S(2)}) copy-start(s32[2048,1]{0,1:T(1,128)} %get-tuple-element.87) | copy-start | bytes 24580
  171.3 9.6 %copy-start.29 = (s32[2048,1]{0,1:T(1,128)S(1)}, s32[2048,1]{0,1:T(1,128)}, u32[]{:S(2)}) copy-start(s32[2048,1]{0,1:T(1,128)} %get-tuple-element.88) | copy-start | bytes 24580
  171.3 9.6 %copy-start.30 = (s32[2048,1]{0,1:T(1,128)S(1)}, s32[2048,1]{0,1:T(1,128)}, u32[]{:S(2)}) copy-start(s32[2048,1]{0,1:T(1,128)} %get-tuple-element.89) | copy-start | bytes 24580
  171.3 9.6 %copy-start.31 = (s32[2048,1]{0,1:T(1,128)S(1)}, s32[2048,1]{0,1:T(1,128)}, u32[]{:S(2)}) copy-start(s32[2048,1]{0,1:T(1,128)} %get-tuple-element.90) | copy-start | bytes 24580
  171.3 9.6 %copy-start.32 = (s32[2048,1]{0,1:T(1,128)S(1)}, s32[2048,1]{0,1:T(1,128)}, u32[]{:S(2)}) copy-start(s32[2048,1]{0,1:T(1,128)} %get-tuple-element.91) | copy-start | bytes 24580
  171.3 9.6 %copy-start.33 = (s32[2048,1]{0,1:T(1,128)S(1)}, s32[2048,1]{0,1:T(1,128)}, u32[]{:S(2)}) copy-start(s32[2048,1]{0,1:T(1,128)} %get-tuple-element.92) | copy-start | bytes 24580
  171.4 9.6 %copy-start.34 = (s32[2048,1]{0,1:T(1,128)S(1)}, s32[2048,1]{0,1:T(1,128)}, u32[]{:S(2)}) copy-start(s32[2048,1]{0,1:T(1,128)} %get-tuple-element.93) | copy-start | bytes 24580
  171.4 9.6 %copy-start.35 = (s32[2048,1]{0,1:T(1,128)S(1)}, s32[2048,1]{0,1:T(1,128)}, u32[]{:S(2)}) copy-start(s32[2048,1]{0,1:T(1,128)} %get-tuple-element.94) | copy-start | bytes 24580
  171.4 9.6 %copy-start.36 = (s32[2048,1]{0,1:T(1,128)S(1)}, s32[2048,1]{0,1:T(1,128)}, u32[]{:S(2)}) copy-start(s32[2048,1]{0,1:T(1,128)} %get-tuple-element.95) | copy-start | bytes 24580
  171.4 9.6 %copy-start.37 = (s32[2048,1]{0,1:T(1,128)S(1)}, s32[2048,1]{0,1:T(1,128)}, u32[]{:S(2)}) copy-start(s32[2048,1]{0,1:T(1,128)} %get-tuple-element.96) | copy-start | bytes 24580
  172.1 8.7 %collective-permute-start.2 = (f32[256,512]{1,0:T(8,128)S(1)}, f32[256,512]{1,0:T(8,128)S(1)}, u32[]{:S(2)}, u32[]{:S(2)}) collective-permute-start(f32[256,512]{1,0:T(8,128)S(1)} %fusion.9), channel_id=1, source_target_pairs={{120,0},{0,8},{8,16},{16,24},{24,32},{32,40},{40,48},{48,56},{56,6... | collective-permute-start | bytes 1572872 | tf_op jit(solution)/shard_map/ppermute | solution.py:13
  186.9 9.1 %collective-permute-start.3 = (f32[256,512]{1,0:T(8,128)S(1)}, f32[256,512]{1,0:T(8,128)S(1)}, u32[]{:S(2)}, u32[]{:S(2)}) collective-permute-start(f32[256,512]{1,0:T(8,128)S(1)} %fusion.8), channel_id=1, source_target_pairs={{120,0},{0,8},{8,16},{16,24},{24,32},{32,40},{40,48},{48,56},{56,6... | collective-permute-start | bytes 1572872 | tf_op jit(solution)/shard_map/ppermute | solution.py:13
  202.0 11.0 %collective-permute-start.4 = (f32[256,512]{1,0:T(8,128)S(1)}, f32[256,512]{1,0:T(8,128)S(1)}, u32[]{:S(2)}, u32[]{:S(2)}) collective-permute-start(f32[256,512]{1,0:T(8,128)S(1)} %fusion.7), channel_id=1, source_target_pairs={{120,0},{0,8},{8,16},{16,24},{24,32},{32,40},{40,48},{48,56},{56,6... | collective-permute-start | bytes 1572872 | tf_op jit(solution)/shard_map/ppermute | solution.py:13
  218.9 10.8 %collective-permute-start.5 = (f32[256,512]{1,0:T(8,128)S(1)}, f32[256,512]{1,0:T(8,128)S(1)}, u32[]{:S(2)}, u32[]{:S(2)}) collective-permute-start(f32[256,512]{1,0:T(8,128)S(1)} %fusion.6), channel_id=1, source_target_pairs={{120,0},{0,8},{8,16},{16,24},{24,32},{32,40},{40,48},{48,56},{56,6... | collective-permute-start | bytes 1572872 | tf_op jit(solution)/shard_map/ppermute | solution.py:13
  235.6 11.0 %collective-permute-start.6 = (f32[256,512]{1,0:T(8,128)S(1)}, f32[256,512]{1,0:T(8,128)S(1)}, u32[]{:S(2)}, u32[]{:S(2)}) collective-permute-start(f32[256,512]{1,0:T(8,128)S(1)} %fusion.5), channel_id=1, source_target_pairs={{120,0},{0,8},{8,16},{16,24},{24,32},{32,40},{40,48},{48,56},{56,6... | collective-permute-start | bytes 1572872 | tf_op jit(solution)/shard_map/ppermute | solution.py:13
  281.6 272.1 %all-reduce.3.cloned.1.call-start = ((), (), s32[]{:S(2)}) async-start(), calls=%async_computation.3 | async-start | bytes 2097152
  (21 other events, 139.9 us)
Sparse Core Ops, SparseCore 0:
  281.7 149.6 reduce-scatter.1
  435.2 118.5 all-reduce.2
